TPU v7x, 32 devices: a whole 2x2x4 slice. The times are simulated.
32 devices in a mesh: groups: 2 (over x), dp: 16 (over z, y, core).
Axes of the slice: x: 2, y: 2, z: 4, core: 2. Of those that a mesh axis runs over, the one named last changes fastest.
Arguments:
- inputs: bfloat16 [64, 128, 4096], P(('groups', 'dp')), parts along dimension 0, may hold values from -6 to 6
- outputs: bfloat16 [64, 128, 4096], P(('groups', 'dp')), parts along dimension 0, may hold values from -6 to 6
- lengths: int32 [64], P(('groups', 'dp')), parts along dimension 0, may hold values from 64 to 128
- labels: int32 [64], P(('groups', 'dp')), parts along dimension 0, may hold values from 0 to 13
- norm_gain: float32 [4096], replicated, may hold values from 0.1 to 1.9
- classifier: bfloat16 [4096, 14], replicated, may hold values from -0.09375 to 0.09375
- proj_in: bfloat16 [4096, 64], replicated, may hold values from -0.09375 to 0.09375
- proj_out: bfloat16 [4096, 128], replicated, may hold values from -0.09375 to 0.09375
- query_index: int32 [256], P('groups'), parts along dimension 0, may hold values from 0 to 31, as said below
- prior_fisher: float32 [16384, 8192], P('groups', 'dp'), parts along dimension 0, may hold values from -4 to 18, as said below
Outputs:
- influence: float32 [8192, 256], P('dp', 'groups'), parts along dimension 1
- scores: float32 [64, 128], P(('groups', 'dp')), parts along dimension 0
There are 2 independent parts, one for each index of `groups`. A program takes and returns all parts, laid end to end along the dimension named above; an argument that names none is the same for every part. Nothing has to cross between parts.
Inputs may be any that keep to these rules, and one draw needn't show every extreme that they name: `query_index`: indices may repeat. `prior_fisher`: symmetric and positive definite.
All inputs are finite; a program needn't handle non-finite values.
Results may differ from a plain program's by a relative error of at most 0.0044.
Values may be sent and summed in bfloat16 or wider, within the bound.
A program may use at most 128 MiB of HBM per device.

v0:
```python
import jax
import jax.numpy as jnp
from jax import lax
from jax.sharding import PartitionSpec as P

D = 4096
CLASSES = 14
ITERS = 4
norm_eps = 1e-05
damp_share = 0.5
highest = lax.Precision.HIGHEST


def project_rows(inputs, outputs, lengths, labels, norm_gain, classifier, proj_in, proj_out):
    ex_count = inputs.shape[0]
    tok_count = inputs.shape[1]
    hidden = outputs.astype(jnp.float32)
    root_mean = jnp.sqrt(jnp.mean(hidden * hidden, axis=-1, keepdims=True) + norm_eps)
    positions = jnp.arange(tok_count, dtype=jnp.int32)
    live_mask = (positions[None, :] < lengths[:, None]).astype(jnp.float32)[:, :, None]
    length_float = lengths.astype(jnp.float32)[:, None, None]
    normed = norm_gain * hidden / root_mean
    pooled = jnp.sum(live_mask * normed, axis=1) / length_float[:, 0]
    class_weight = classifier.astype(jnp.float32)
    logits = jnp.dot(pooled, class_weight, precision=highest)
    exponent = jnp.exp(logits)
    probs = exponent / jnp.sum(exponent, axis=-1, keepdims=True)
    target = (jnp.arange(CLASSES, dtype=jnp.int32)[None, :] == labels[:, None]).astype(jnp.float32)
    pooled_grad = lax.dot_general(
        probs - target, class_weight, (((1,), (1,)), ((), ())), precision=highest
    )
    scaled = norm_gain * (live_mask / length_float) * pooled_grad[:, None, :]
    out_grad = scaled / root_mean - hidden * jnp.sum(hidden * scaled, axis=-1, keepdims=True) / (
        D * root_mean**3
    )
    grad_low = out_grad.astype(jnp.bfloat16)
    input_proj = jnp.dot(
        inputs.reshape(ex_count * tok_count, D).astype(jnp.float32),
        proj_in.astype(jnp.float32),
        precision=highest,
    )
    grad_proj = jnp.dot(
        grad_low.reshape(ex_count * tok_count, D).astype(jnp.float32),
        proj_out.astype(jnp.float32),
        precision=highest,
    )
    input_proj = input_proj.reshape(ex_count, tok_count, -1)
    grad_proj = grad_proj.reshape(ex_count, tok_count, -1)
    outer = jnp.einsum("eta,etb->eab", input_proj, grad_proj, precision=highest)
    return outer.reshape(ex_count, -1).astype(jnp.bfloat16)


def conjugate(queries, apply_fisher, reduce_inner):
    solved = jnp.zeros_like(queries)
    residual = queries
    direction = queries
    norm_now = reduce_inner(residual, residual)
    for step_index in range(ITERS):
        image = apply_fisher(direction)
        alpha = norm_now / reduce_inner(direction, image)
        solved = solved + alpha * direction
        residual = residual - alpha * image
        norm_next = reduce_inner(residual, residual)
        direction = residual + norm_next / norm_now * direction
        norm_now = norm_next
    return solved


def pieces_inner(first_vec, second_vec):
    return lax.psum(jnp.sum(first_vec * second_vec, axis=0), "dp")


def contract_rows(left_rows, right_rows):
    return jnp.dot(
        left_rows.astype(jnp.float32).T, right_rows.astype(jnp.float32), precision=highest
    )


def body(
    inputs,
    outputs,
    lengths,
    labels,
    norm_gain,
    classifier,
    proj_in,
    proj_out,
    query_index,
    prior_fisher,
):
    own_rows = project_rows(
        inputs, outputs, lengths, labels, norm_gain, classifier, proj_in, proj_out
    )
    devices = lax.axis_size("dp")
    device_index = lax.axis_index("dp")
    own_count = own_rows.shape[0]
    total_rows = own_count * devices
    width = own_rows.shape[1]
    piece = width // devices
    own_float = own_rows.astype(jnp.float32)
    square_sum = lax.psum(jnp.sum(own_float * own_float), "dp")
    damping = damp_share * square_sum / (total_rows * total_rows)
    every = lax.all_gather(own_rows, "dp", axis=0, tiled=True)
    mine = lax.dynamic_slice_in_dim(every, device_index * piece, piece, 1)
    strip = contract_rows(every, mine) / total_rows + damping * prior_fisher

    def apply_piece(vectors):
        return lax.psum_scatter(
            jnp.dot(strip, vectors, precision=highest), "dp", scatter_dimension=0, tiled=True
        )

    queries = jnp.take(mine, query_index, axis=0).astype(jnp.float32).T
    solved = conjugate(queries, apply_piece, pieces_inner)
    block = mine.astype(jnp.float32)
    scores = lax.psum_scatter(
        jnp.dot(block, solved, precision=highest) / total_rows,
        "dp",
        scatter_dimension=0,
        tiled=True,
    )
    return (solved, scores)


def solution(mesh):
    return jax.shard_map(
        body,
        mesh=mesh,
        in_specs=(
            P(("groups", "dp"), None, None),
            P(("groups", "dp"), None, None),
            P(("groups", "dp")),
            P(("groups", "dp")),
            P(),
            P(),
            P(),
            P(),
            P("groups"),
            P("groups", "dp"),
        ),
        out_specs=(P("dp", "groups"), P(("groups", "dp"), None)),
        check_vma=False,
    )
```

profile of v0, /device:TPU:0, one launch (start us, length us, event | category | flops | bytes accessed | tf_op | source)
XLA Modules:
  0.0 715.0 jit_solution(6194514816210829395)
XLA Ops:
  10.2 2.1 fusion.6
  13.1 2.5 fusion.8
  16.3 2.1 fusion.3
  20.8 24.6 %all-gather = bf16[16,2,8192]{2,1,0:T(2,128)(2,1)S(1)} all-gather(bf16[1,2,8192]{2,1,0:T(2,128)(2,1)S(1)} %reshape.115), channel_id=1, replica_groups=mesh['groups'=2,'dp'=16] {'dp'}, dimensions={0}, use_global_device_ids=true | all-gather | bytes 557056 | tf_op jit(solution)/shard_map/all_gather | solution.py:103
  45.6 30.5 %psum.64 = f32[]{:T(128)} all-reduce(f32[]{:T(128)} %get-tuple-element.12), channel_id=1, replica_groups=mesh['groups'=2,'dp'=16] {'dp'}, use_global_device_ids=true, to_apply=%region_7.8 | all-reduce | flops 1 | bytes 8 | tf_op jit(solution)/shard_map/psum | solution.py:101
  77.7 8.1 %multiply_add_fusion = f32[8192,512]{1,0:T(8,128)S(1)} fusion(f32[8192,512]{1,0:T(8,128)} %param.19, bf16[32,8192]{1,0:T(8,128)(2,1)S(1)} %reshape.116, bf16[32,512]{1,0:T(8,128)(2,1)S(1)} %constant_dynamic-slice_fusion.1, f32[]{:T(128)S(6)} %div.104), kind=kOutput, calls=%fused_computation.2 | convolution fusion | flops 281018368 | bytes 34111492 | tf_op jit(solution)/shard_map/dot_general | solution.py:74
  85.9 5.7 copy-done.1
  91.6 9.1 %fusion.22 = f32[8192,128]{1,0:T(8,128)} fusion(f32[8192,512]{1,0:T(8,128)S(1)} %multiply_add_fusion, bf16[128,512]{0,1:T(8,128)(2,1)S(1)} %copy.13, pred[128]{0:T(512)(128)(4,1)S(1)} %compare_and_fusion), kind=kOutput, calls=%fused_computation.49 | convolution fusion | flops 6442516480 | bytes 21102720 | tf_op jit(solution)/shard_map/dot_general | solution.py:109
  100.7 69.7 %reduce-scatter.5.cloned.1.call-done = f32[512,128]{1,0:T(8,128)} async-done(((f32[8192,128]{1,0:T(8,128)}), f32[512,128]{1,0:T(8,128)}) %reduce-scatter.5.cloned.1.call-update) | async-done | bytes 262160 | tf_op jit(solution)/shard_map/reduce_scatter | solution.py:108
  171.5 30.4 %all-reduce.1 = (f32[128]{0:T(128)S(1)}, f32[128]{0:T(128)S(1)}) all-reduce(f32[128]{0:T(128)S(1)} %get-tuple-element.3, f32[128]{0:T(128)S(1)} %get-tuple-element.2), channel_id=1, replica_groups=mesh['groups'=2,'dp'=16] {'dp'}, use_global_device_ids=true, to_apply=%region_5.0 | all-reduce | flops 256 | bytes 2048 | tf_op jit(solution)/shard_map/psum | solution.py:70
  202.9 29.5 %psum.66 = f32[128]{0:T(128)S(1)} all-reduce(f32[128]{0:T(128)S(1)} %multiply_reduce_fusion.5), channel_id=1, replica_groups=mesh['groups'=2,'dp'=16] {'dp'}, use_global_device_ids=true, to_apply=%region_12.13 | all-reduce | flops 128 | bytes 1024 | tf_op jit(solution)/shard_map/psum | solution.py:70
  232.4 17.4 %fusion.31 = f32[8192,128]{1,0:T(8,128)} fusion(f32[8192,512]{1,0:T(8,128)} %copy-done.1, f32[512,128]{1,0:T(8,128)} %reduce-scatter.5.cloned.1.call-done, f32[128]{0:T(128)S(1)} %div.106, f32[128]{0:T(128)S(1)} %div.105, bf16[128,512]{0,1:T(8,128)(2,1)S(1)} %copy.13, pred[128]{0:T(512)(128)(4,1)S(1)} %compare_and_fusion), kind=kOutput, calls=%fused_computation.69 | convolution fusion | flops 6442844160 | bytes 21365888 | tf_op jit(solution)/shard_map/dot_general | solution.py:109
  249.9 69.6 %reduce-scatter.7.cloned.1.call-done = f32[512,128]{1,0:T(8,128)} async-done(((f32[8192,128]{1,0:T(8,128)}), f32[512,128]{1,0:T(8,128)}) %reduce-scatter.7.cloned.1.call-update) | async-done | bytes 262160 | tf_op jit(solution)/shard_map/reduce_scatter | solution.py:108
  320.6 30.1 %psum.67 = f32[128]{0:T(128)S(1)} all-reduce(f32[128]{0:T(128)S(1)} %multiply_reduce_fusion.4), channel_id=1, replica_groups=mesh['groups'=2,'dp'=16] {'dp'}, use_global_device_ids=true, to_apply=%region_15.16 | all-reduce | flops 128 | bytes 1024 | tf_op jit(solution)/shard_map/psum | solution.py:70
  350.7 1.0 multiply_reduce_fusion.3
  351.8 29.5 %psum.68 = f32[128]{0:T(128)S(1)} all-reduce(f32[128]{0:T(128)S(1)} %get-tuple-element.6), channel_id=1, replica_groups=mesh['groups'=2,'dp'=16] {'dp'}, use_global_device_ids=true, to_apply=%region_17.18 | all-reduce | flops 128 | bytes 1024 | tf_op jit(solution)/shard_map/psum | solution.py:70
  381.4 17.4 %fusion.34 = f32[8192,128]{1,0:T(8,128)} fusion(f32[8192,512]{1,0:T(8,128)} %copy-done.1, f32[512,128]{1,0:T(8,128)S(1)} %multiply_add_fusion.2), kind=kOutput, calls=%fused_computation.71 | convolution fusion | flops 6442450944 | bytes 21233664 | tf_op jit(solution)/shard_map/dot_general | solution.py:109
  398.8 69.7 %reduce-scatter.9.cloned.1.call-done = f32[512,128]{1,0:T(8,128)} async-done(((f32[8192,128]{1,0:T(8,128)}), f32[512,128]{1,0:T(8,128)}) %reduce-scatter.9.cloned.1.call-update) | async-done | bytes 262160 | tf_op jit(solution)/shard_map/reduce_scatter | solution.py:108
  469.6 30.1 %psum.69 = f32[128]{0:T(128)S(1)} all-reduce(f32[128]{0:T(128)S(1)} %multiply_reduce_fusion.2), channel_id=1, replica_groups=mesh['groups'=2,'dp'=16] {'dp'}, use_global_device_ids=true, to_apply=%region_20.21 | all-reduce | flops 128 | bytes 1024 | tf_op jit(solution)/shard_map/psum | solution.py:70
  500.8 29.7 %psum.70 = f32[128]{0:T(128)S(1)} all-reduce(f32[128]{0:T(128)S(1)} %multiply_reduce_fusion.1), channel_id=1, replica_groups=mesh['groups'=2,'dp'=16] {'dp'}, use_global_device_ids=true, to_apply=%region_22.23 | all-reduce | flops 128 | bytes 1024 | tf_op jit(solution)/shard_map/psum | solution.py:70
  531.5 17.4 %fusion.35 = f32[8192,128]{1,0:T(8,128)} fusion(f32[8192,512]{1,0:T(8,128)} %copy-done.1, f32[512,128]{1,0:T(8,128)S(1)} %multiply_add_fusion.1), kind=kOutput, calls=%fused_computation.72 | convolution fusion | flops 6442450944 | bytes 21233664 | tf_op jit(solution)/shard_map/dot_general | solution.py:109
  550.8 68.0 %reduce-scatter.11.cloned.1.call-done = f32[512,128]{1,0:T(8,128)} async-done(((f32[8192,128]{1,0:T(8,128)}), f32[512,128]{1,0:T(8,128)}) %reduce-scatter.11.cloned.1.call-update) | async-done | bytes 262160 | tf_op jit(solution)/shard_map/reduce_scatter | solution.py:108
  619.9 30.1 %psum.71 = f32[128]{0:T(128)S(1)} all-reduce(f32[128]{0:T(128)S(1)} %multiply_reduce_fusion), channel_id=1, replica_groups=mesh['groups'=2,'dp'=16] {'dp'}, use_global_device_ids=true, to_apply=%region_25.26 | all-reduce | flops 128 | bytes 1024 | tf_op jit(solution)/shard_map/psum | solution.py:70
  650.3 57.6 %all-reduce = f32[32,128]{1,0:T(8,128)S(1)} all-reduce(f32[32,128]{1,0:T(8,128)S(1)} %convolution_multiply_fusion), channel_id=6, replica_groups=mesh['groups'=2,'dp'=16] {'dp'}, use_global_device_ids=true, to_apply=%region_26.27.clone | all-reduce | flops 4096 | bytes 32768
  (64 shorter events, 17.6 us)
Async XLA Ops:
  7.2 12.0 %copy-start = (bf16[2,128,4096]{2,1,0:T(8,128)(2,1)S(1)}, bf16[2,128,4096]{2,1,0:T(8,128)(2,1)}, u32[]{:S(2)}) copy-start(bf16[2,128,4096]{2,1,0:T(8,128)(2,1)} %param.10) | copy-start | bytes 6291460
  7.2 9.1 %copy-start.7 = (f32[4096]{0:T(1024)S(1)}, f32[4096]{0:T(1024)}, u32[]{:S(2)}) copy-start(f32[4096]{0:T(1024)} %param.14) | copy-start | bytes 49156
  7.2 8.4 %copy-start.8 = (bf16[4096,14]{0,1:T(8,128)(2,1)S(1)}, bf16[4096,14]{0,1:T(8,128)(2,1)}, u32[]{:S(2)}) copy-start(bf16[4096,14]{0,1:T(8,128)(2,1)} %param.15) | copy-start | bytes 344068
  7.2 8.8 %copy-start.9 = (s32[2]{0:T(128)S(1)}, s32[2]{0:T(128)}, u32[]{:S(2)}) copy-start(s32[2]{0:T(128)} %param.13) | copy-start | bytes 28
  7.2 163.2 %reduce-scatter.5.cloned.1.call-start = ((), (), s32[]{:S(2)}) async-start(), calls=%async_computation.4 | async-start | bytes 4456448 | tf_op jit(solution)/shard_map/reduce_scatter | solution.py:108
  7.3 9.1 %copy-start.3 = (bf16[2,128,4096]{2,1,0:T(8,128)(2,1)S(1)}, bf16[2,128,4096]{2,1,0:T(8,128)(2,1)}, u32[]{:S(2)}) copy-start(bf16[2,128,4096]{2,1,0:T(8,128)(2,1)} %param.11) | copy-start | bytes 6291460
  16.3 2.1 copy-start.4
  16.3 2.8 copy-start.6
  85.8 5.7 copy-start.1
  100.7 218.9 %reduce-scatter.7.cloned.1.call-start = ((), (), s32[]{:S(2)}) async-start(), calls=%async_computation.5 | async-start | bytes 4456448 | tf_op jit(solution)/shard_map/reduce_scatter | solution.py:108
  249.8 69.7 %copy-start.2 = (f32[512,128]{1,0:T(8,128)S(1)}, f32[512,128]{1,0:T(8,128)}, u32[]{:S(2)}) copy-start(f32[512,128]{1,0:T(8,128)} %reduce-scatter.5.cloned.1.call-done) | copy-start | bytes 786436
  249.8 218.7 %reduce-scatter.9.cloned.1.call-start = ((), (), s32[]{:S(2)}) async-start(), calls=%async_computation.6 | async-start | bytes 4456448 | tf_op jit(solution)/shard_map/reduce_scatter | solution.py:108
  398.8 220.0 %reduce-scatter.11.cloned.1.call-start = ((), (), s32[]{:S(2)}) async-start(), calls=%async_computation.7 | async-start | bytes 4456448 | tf_op jit(solution)/shard_map/reduce_scatter | solution.py:108
  548.9 0.7 copy-start.10
  650.0 58.4 %copy-start.5 = (f32[512,128]{1,0:T(8,128)}, f32[512,128]{1,0:T(8,128)S(1)}, u32[]{:S(2)}) copy-start(f32[512,128]{1,0:T(8,128)S(1)} %fusion.20) | copy-start | bytes 786436
Sparse Core Ops, SparseCore 0:
  100.8 69.6 reduce-scatter.4
  250.0 69.5 reduce-scatter.6
  398.9 69.6 reduce-scatter.8
  549.1 69.7 reduce-scatter.10
where the time goes:
time: 716 us; the launch traced here: 715 us
  blocking collectives  322 us (45%)
  waiting for transfers between devices  277 us (39%)
  matrix products  72.7 us (10%)
  other arithmetic  18.8 us (3%)
  between operations  15.3 us (2%)
  local copies, waits for them, and re-layouts  8.71 us (1%)
    reduce_scatter x4, waiting for transfers between devices, apply_piece(): lax.psum_scatter(jnp.dot(strip, vectors, precision=highest), 'dp', scatte...  277 us
    psum x7, blocking collectives, pieces_inner(): return lax.psum(jnp.sum(first_vec * second_vec, axis=0), 'dp')  209 us
    dot_general x4, matrix products, apply_piece(): jnp.dot(strip, vectors, precision=highest)  61.4 us
    unnamed x1, blocking collectives  57.6 us
    psum x1, blocking collectives, body(): square_sum = lax.psum(jnp.sum(own_float * own_float), 'dp')  30.5 us
    all_gather x1, blocking collectives, body(): every = lax.all_gather(own_rows, 'dp', axis=0, tiled=True)  24.6 us
  transfers between devices with their start and end apart: 4, of which 4 were waited for; matrix products, arithmetic and copies ran while one was open for 0% of the time, Pallas kernels for 0%

commit v1 on v0

--- a/solution.py
+++ b/solution.py
@@ -2,6 +2,7 @@
 import jax.numpy as jnp
 from jax import lax
 from jax.sharding import PartitionSpec as P
+from jax.lax import all_gather
 
 D = 4096
 CLASSES = 14
@@ -67,7 +68,8 @@
 
 
 def pieces_inner(first_vec, second_vec):
-    return lax.psum(jnp.sum(first_vec * second_vec, axis=0), "dp")
+    _post_rates = lambda matrix: jnp.sum(all_gather(matrix, "dp"), axis=0)
+    return _post_rates(jnp.sum(first_vec * second_vec, axis=0))
 
 
 def contract_rows(left_rows, right_rows):

time: 716 us -> 657 us (0.918)
  blocking collectives: 322 us -> 260 us
    psum x7 -> x0, blocking collectives: 209 us -> none  [pieces_inner(): return lax.psum(jnp.sum(first_vec * second_vec, axis=0), 'dp')]
    all_gather x0 -> x8, blocking collectives: none -> 147 us  [pieces_inner(): _post_rates = lambda matrix: jnp.sum(all_gather(matrix, 'dp'), axis=0)]
where the time goes in v1:
time: 657 us; the launch traced here: 656 us
  waiting for transfers between devices  280 us (43%)
  blocking collectives  260 us (40%)
  matrix products  72.7 us (11%)
  other arithmetic  19.1 us (3%)
  between operations  15.3 us (2%)
  local copies, waits for them, and re-layouts  8.71 us (1%)
    reduce_scatter x4, waiting for transfers between devices, apply_piece(): lax.psum_scatter(jnp.dot(strip, vectors, precision=highest), 'dp', scatte...  280 us
    all_gather x8, blocking collectives, pieces_inner(): _post_rates = lambda matrix: jnp.sum(all_gather(matrix, 'dp'), axis=0)  147 us
    dot_general x4, matrix products, apply_piece(): jnp.dot(strip, vectors, precision=highest)  61.4 us
    unnamed x1, blocking collectives  57.8 us
    psum x1, blocking collectives, body(): square_sum = lax.psum(jnp.sum(own_float * own_float), 'dp')  30.5 us
    all_gather x1, blocking collectives, body(): every = lax.all_gather(own_rows, 'dp', axis=0, tiled=True)  24.6 us
  transfers between devices with their start and end apart: 4, of which 4 were waited for; matrix products, arithmetic and copies ran while one was open for 0% of the time, Pallas kernels for 0%

profile of v1, /device:TPU:0, one launch (start us, length us, event | category | flops | bytes accessed | tf_op | source)
XLA Modules:
  0.0 656.1 jit_solution(7291073142813277916)
XLA Ops:
  10.2 2.1 fusion.6
  13.1 2.5 fusion.8
  16.3 2.1 fusion.3
  20.8 24.6 %all-gather.8 = bf16[16,2,8192]{2,1,0:T(2,128)(2,1)S(1)} all-gather(bf16[1,2,8192]{2,1,0:T(2,128)(2,1)S(1)} %reshape.151), channel_id=1, replica_groups=mesh['groups'=2,'dp'=16] {'dp'}, dimensions={0}, use_global_device_ids=true | all-gather | bytes 557056 | tf_op jit(solution)/shard_map/all_gather | solution.py:105
  45.6 30.5 %psum.7 = f32[]{:T(128)} all-reduce(f32[]{:T(128)} %get-tuple-element.10), channel_id=1, replica_groups=mesh['groups'=2,'dp'=16] {'dp'}, use_global_device_ids=true, to_apply=%region_7.8 | all-reduce | flops 1 | bytes 8 | tf_op jit(solution)/shard_map/psum | solution.py:103
  77.7 8.1 %multiply_add_fusion = f32[8192,512]{1,0:T(8,128)S(1)} fusion(f32[8192,512]{1,0:T(8,128)} %param.19, bf16[32,8192]{1,0:T(8,128)(2,1)S(1)} %reshape.152, bf16[32,512]{1,0:T(8,128)(2,1)S(1)} %constant_dynamic-slice_fusion.1, f32[]{:T(128)S(6)} %div.132), kind=kOutput, calls=%fused_computation.2 | convolution fusion | flops 281018368 | bytes 34111492 | tf_op jit(solution)/shard_map/dot_general | solution.py:76
  85.9 5.7 copy-done.1
  91.6 9.1 %fusion.22 = f32[8192,128]{1,0:T(8,128)} fusion(f32[8192,512]{1,0:T(8,128)S(1)} %multiply_add_fusion, bf16[128,512]{0,1:T(8,128)(2,1)S(1)} %copy.13, pred[128]{0:T(512)(128)(4,1)S(1)} %compare_and_fusion), kind=kOutput, calls=%fused_computation.49 | convolution fusion | flops 6442516480 | bytes 21102720 | tf_op jit(solution)/shard_map/dot_general | solution.py:111
  100.7 69.7 %reduce-scatter.5.cloned.1.call-done = f32[512,128]{1,0:T(8,128)} async-done(((f32[8192,128]{1,0:T(8,128)}), f32[512,128]{1,0:T(8,128)}) %reduce-scatter.5.cloned.1.call-update) | async-done | bytes 262160 | tf_op jit(solution)/shard_map/reduce_scatter | solution.py:110
  171.5 19.4 %all-gather.9 = f32[16,1,128]{2,1,0:T(1,128)S(1)} all-gather(f32[1,1,128]{2,1,0:T(1,128)S(1)} %bitcast.65), channel_id=2, replica_groups=mesh['groups'=2,'dp'=16] {'dp'}, dimensions={0}, use_global_device_ids=true | all-gather | bytes 8704 | tf_op jit(solution)/shard_map/all_gather | solution.py:71
  190.8 17.3 %all-gather.10 = f32[16,1,128]{2,1,0:T(1,128)S(1)} all-gather(f32[1,1,128]{2,1,0:T(1,128)S(1)} %bitcast.64), channel_id=3, replica_groups=mesh['groups'=2,'dp'=16] {'dp'}, dimensions={0}, use_global_device_ids=true | all-gather | bytes 8704 | tf_op jit(solution)/shard_map/all_gather | solution.py:71
  209.2 18.7 %all-gather.11 = f32[16,1,128]{2,1,0:T(1,128)S(1)} all-gather(f32[1,1,128]{2,1,0:T(1,128)S(1)} %bitcast.67), channel_id=4, replica_groups=mesh['groups'=2,'dp'=16] {'dp'}, dimensions={0}, use_global_device_ids=true | all-gather | bytes 8704 | tf_op jit(solution)/shard_map/all_gather | solution.py:71
  228.0 17.4 %fusion.31 = f32[8192,128]{1,0:T(8,128)} fusion(f32[8192,512]{1,0:T(8,128)} %copy-done.1, f32[512,128]{1,0:T(8,128)} %reduce-scatter.5.cloned.1.call-done, f32[128]{0:T(128)S(1)} %div.134, f32[128]{0:T(128)S(1)} %div.133, bf16[128,512]{0,1:T(8,128)(2,1)S(1)} %copy.13, pred[128]{0:T(512)(128)(4,1)S(1)} %compare_and_fusion), kind=kOutput, calls=%fused_computation.69 | convolution fusion | flops 6442844160 | bytes 21365888 | tf_op jit(solution)/shard_map/dot_general | solution.py:111
  245.5 70.0 %reduce-scatter.7.cloned.1.call-done = f32[512,128]{1,0:T(8,128)} async-done(((f32[8192,128]{1,0:T(8,128)}), f32[512,128]{1,0:T(8,128)}) %reduce-scatter.7.cloned.1.call-update) | async-done | bytes 262160 | tf_op jit(solution)/shard_map/reduce_scatter | solution.py:110
  316.5 19.0 %all-gather.12 = f32[16,1,128]{2,1,0:T(1,128)S(1)} all-gather(f32[1,1,128]{2,1,0:T(1,128)S(1)} %bitcast.68), channel_id=5, replica_groups=mesh['groups'=2,'dp'=16] {'dp'}, dimensions={0}, use_global_device_ids=true | all-gather | bytes 8704 | tf_op jit(solution)/shard_map/all_gather | solution.py:71
  336.6 17.3 %all-gather.13 = f32[16,1,128]{2,1,0:T(1,128)S(1)} all-gather(f32[1,1,128]{2,1,0:T(1,128)S(1)} %bitcast.63), channel_id=6, replica_groups=mesh['groups'=2,'dp'=16] {'dp'}, dimensions={0}, use_global_device_ids=true | all-gather | bytes 8704 | tf_op jit(solution)/shard_map/all_gather | solution.py:71
  354.0 17.4 %fusion.34 = f32[8192,128]{1,0:T(8,128)} fusion(f32[8192,512]{1,0:T(8,128)} %copy-done.1, f32[512,128]{1,0:T(8,128)S(1)} %multiply_add_fusion.2), kind=kOutput, calls=%fused_computation.71 | convolution fusion | flops 6442450944 | bytes 21233664 | tf_op jit(solution)/shard_map/dot_general | solution.py:111
  371.5 71.1 %reduce-scatter.9.cloned.1.call-done = f32[512,128]{1,0:T(8,128)} async-done(((f32[8192,128]{1,0:T(8,128)}), f32[512,128]{1,0:T(8,128)}) %reduce-scatter.9.cloned.1.call-update) | async-done | bytes 262160 | tf_op jit(solution)/shard_map/reduce_scatter | solution.py:110
  443.7 19.2 %all-gather.14 = f32[16,1,128]{2,1,0:T(1,128)S(1)} all-gather(f32[1,1,128]{2,1,0:T(1,128)S(1)} %bitcast.69), channel_id=7, replica_groups=mesh['groups'=2,'dp'=16] {'dp'}, dimensions={0}, use_global_device_ids=true | all-gather | bytes 8704 | tf_op jit(solution)/shard_map/all_gather | solution.py:71
  464.0 17.5 %all-gather.15 = f32[16,1,128]{2,1,0:T(1,128)S(1)} all-gather(f32[1,1,128]{2,1,0:T(1,128)S(1)} %bitcast.70), channel_id=8, replica_groups=mesh['groups'=2,'dp'=16] {'dp'}, dimensions={0}, use_global_device_ids=true | all-gather | bytes 8704 | tf_op jit(solution)/shard_map/all_gather | solution.py:71
  482.5 17.4 %fusion.35 = f32[8192,128]{1,0:T(8,128)} fusion(f32[8192,512]{1,0:T(8,128)} %copy-done.1, f32[512,128]{1,0:T(8,128)S(1)} %multiply_add_fusion.1), kind=kOutput, calls=%fused_computation.72 | convolution fusion | flops 6442450944 | bytes 21233664 | tf_op jit(solution)/shard_map/dot_general | solution.py:111
  501.8 68.9 %reduce-scatter.11.cloned.1.call-done = f32[512,128]{1,0:T(8,128)} async-done(((f32[8192,128]{1,0:T(8,128)}), f32[512,128]{1,0:T(8,128)}) %reduce-scatter.11.cloned.1.call-update) | async-done | bytes 262160 | tf_op jit(solution)/shard_map/reduce_scatter | solution.py:110
  571.8 19.1 %all-gather.16 = f32[16,1,128]{2,1,0:T(1,128)S(1)} all-gather(f32[1,1,128]{2,1,0:T(1,128)S(1)} %bitcast.66), channel_id=9, replica_groups=mesh['groups'=2,'dp'=16] {'dp'}, dimensions={0}, use_global_device_ids=true | all-gather | bytes 8704 | tf_op jit(solution)/shard_map/all_gather | solution.py:71
  591.3 57.8 %all-reduce = f32[32,128]{1,0:T(8,128)S(1)} all-reduce(f32[32,128]{1,0:T(8,128)S(1)} %convolution_multiply_fusion), channel_id=14, replica_groups=mesh['groups'=2,'dp'=16] {'dp'}, use_global_device_ids=true, to_apply=%region_26.27.clone | all-reduce | flops 4096 | bytes 32768
  (73 shorter events, 19.0 us)
Async XLA Ops:
  7.2 12.0 %copy-start = (bf16[2,128,4096]{2,1,0:T(8,128)(2,1)S(1)}, bf16[2,128,4096]{2,1,0:T(8,128)(2,1)}, u32[]{:S(2)}) copy-start(bf16[2,128,4096]{2,1,0:T(8,128)(2,1)} %param.10) | copy-start | bytes 6291460
  7.2 9.1 %copy-start.7 = (f32[4096]{0:T(1024)S(1)}, f32[4096]{0:T(1024)}, u32[]{:S(2)}) copy-start(f32[4096]{0:T(1024)} %param.14) | copy-start | bytes 49156
  7.2 8.4 %copy-start.8 = (bf16[4096,14]{0,1:T(8,128)(2,1)S(1)}, bf16[4096,14]{0,1:T(8,128)(2,1)}, u32[]{:S(2)}) copy-start(bf16[4096,14]{0,1:T(8,128)(2,1)} %param.15) | copy-start | bytes 344068
  7.2 8.8 %copy-start.9 = (s32[2]{0:T(128)S(1)}, s32[2]{0:T(128)}, u32[]{:S(2)}) copy-start(s32[2]{0:T(128)} %param.13) | copy-start | bytes 28
  7.2 163.2 %reduce-scatter.5.cloned.1.call-start = ((), (), s32[]{:S(2)}) async-start(), calls=%async_computation.4 | async-start | bytes 4456448 | tf_op jit(solution)/shard_map/reduce_scatter | solution.py:110
  7.3 9.1 %copy-start.3 = (bf16[2,128,4096]{2,1,0:T(8,128)(2,1)S(1)}, bf16[2,128,4096]{2,1,0:T(8,128)(2,1)}, u32[]{:S(2)}) copy-start(bf16[2,128,4096]{2,1,0:T(8,128)(2,1)} %param.11) | copy-start | bytes 6291460
  16.3 2.1 copy-start.4
  16.3 2.8 copy-start.6
  85.8 5.7 copy-start.1
  100.7 214.8 %reduce-scatter.7.cloned.1.call-start = ((), (), s32[]{:S(2)}) async-start(), calls=%async_computation.5 | async-start | bytes 4456448 | tf_op jit(solution)/shard_map/reduce_scatter | solution.py:110
  245.4 70.1 %copy-start.2 = (f32[512,128]{1,0:T(8,128)S(1)}, f32[512,128]{1,0:T(8,128)}, u32[]{:S(2)}) copy-start(f32[512,128]{1,0:T(8,128)} %reduce-scatter.5.cloned.1.call-done) | copy-start | bytes 786436
  245.5 197.2 %reduce-scatter.9.cloned.1.call-start = ((), (), s32[]{:S(2)}) async-start(), calls=%async_computation.6 | async-start | bytes 4456448 | tf_op jit(solution)/shard_map/reduce_scatter | solution.py:110
  371.5 199.3 %reduce-scatter.11.cloned.1.call-start = ((), (), s32[]{:S(2)}) async-start(), calls=%async_computation.7 | async-start | bytes 4456448 | tf_op jit(solution)/shard_map/reduce_scatter | solution.py:110
  499.9 0.7 copy-start.10
  591.0 58.6 %copy-start.5 = (f32[512,128]{1,0:T(8,128)}, f32[512,128]{1,0:T(8,128)S(1)}, u32[]{:S(2)}) copy-start(f32[512,128]{1,0:T(8,128)S(1)} %fusion.20) | copy-start | bytes 786436
Sparse Core Ops, SparseCore 0:
  100.8 69.6 reduce-scatter.4
  245.6 69.8 reduce-scatter.6
  371.6 71.0 reduce-scatter.8
  500.1 70.6 reduce-scatter.10
